TPU v7x, 256 devices: a whole 4x4x8 slice. The times are simulated.
256 devices in a mesh: seq: 64 (over z, y, core), grp: 4 (over x).
Axes of the slice: x: 4, y: 4, z: 8, core: 2. Of those that a mesh axis runs over, the one named last changes fastest.
Arguments:
- q_nope: bfloat16 [1024, 128, 128], P('seq', 'grp'), may hold values from -6 to 6
- q_rope: bfloat16 [1024, 128, 64], P('seq', 'grp'), may hold values from -256 to 256
- cache: bfloat16 [65536, 576], P('seq'), may hold values from -6 to 6
- w_uk: bfloat16 [128, 65536], P('grp', 'seq'), may hold values from -0.5 to 0.5
- w_uv: bfloat16 [128, 65536], P('grp', 'seq'), may hold values from -0.25 to 0.25
- d_out: bfloat16 [1024, 128, 128], P('seq', 'grp'), may hold values from -6 to 6
- sel: int32 [1024, 32], P('seq'), may hold values from 0 to 63, as said below
- slot_blocks: int32 [64, 64], P('seq'), may hold values from 0 to 15, as said below
Outputs:
- attn_out: bfloat16 [1024, 128, 128], P('seq', 'grp')
- d_q_nope: bfloat16 [1024, 128, 128], P('seq', 'grp')
- d_q_rope: bfloat16 [1024, 128, 64], P('seq', 'grp')
- d_cache: float32 [65536, 576], P('seq')
Inputs may be any that keep to these rules, and one draw needn't show every extreme that they name: `sel`: each row names 32 different places; place s stands for the block that the row's device asks of device s. `slot_blocks`: entry [r, s] is the index among device s's own blocks of the block that device r asks for in place s; the 1 entries of a row toward one device differ.
All inputs are finite; a program needn't handle non-finite values.
Results may differ from a plain program's by a relative error of at most 0.015.
Values may be sent and summed in bfloat16 or wider, within the bound.
A program may use at most 128 MiB of HBM per device.

v0:
```python
import math
import jax
import jax.numpy as jnp
from jax import lax
from jax.sharding import PartitionSpec as P

BLOCK_LEN = 64


def local(q_nope, q_rope, cache, w_uk, w_uv, d_out, sel, slot_blocks):
    peers = lax.axis_size("seq")
    queries, heads, nope = q_nope.shape
    rope = q_rope.shape[2]
    width = cache.shape[1]
    latent = width - rope
    value = d_out.shape[2]
    slot_total = slot_blocks.shape[1]
    per_peer = slot_total // peers
    own_blocks = cache.shape[0] // BLOCK_LEN
    scale = 1.0 / math.sqrt(nope + rope)
    gathered_k, gathered_v = (
        lax.all_gather(w_uk, "seq", axis=1, tiled=True),
        lax.all_gather(w_uv, "seq", axis=1, tiled=True),
    )
    weight_k = gathered_k.reshape(heads, nope, latent)
    weight_v = gathered_v.reshape(heads, latent, value)
    wanted = slot_blocks.reshape(peers, per_peer)
    asked = lax.all_to_all(wanted, "seq", split_axis=0, concat_axis=0, tiled=True)
    blocks = cache.reshape(own_blocks, BLOCK_LEN, width)
    arrived = lax.all_to_all(blocks[asked], "seq", split_axis=0, concat_axis=0, tiled=True)
    keys = arrived.reshape(slot_total * BLOCK_LEN, width)
    keys_lat = keys[:, :latent]
    q_lat = jnp.einsum("qhn,hnl->qhl", q_nope, weight_k, preferred_element_type=jnp.float32).astype(
        jnp.bfloat16
    )
    qfull = jnp.concatenate([q_lat, q_rope], axis=-1)
    chosen = jnp.any(
        sel[:, :, None] == jnp.arange(slot_total, dtype=jnp.int32)[None, None, :], axis=1
    )
    live = jnp.repeat(chosen, BLOCK_LEN, axis=1)[:, None, :]
    score = jnp.einsum("qhc,tc->qht", qfull, keys, preferred_element_type=jnp.float32) * scale
    score = jnp.where(live, score, -jnp.inf)
    prob = jax.nn.softmax(score, axis=-1)
    prob_low = prob.astype(jnp.bfloat16)
    olat = jnp.einsum("qht,tl->qhl", prob_low, keys_lat, preferred_element_type=jnp.float32).astype(
        jnp.bfloat16
    )
    attn_out = jnp.einsum(
        "qhl,hlv->qhv", olat, weight_v, preferred_element_type=jnp.float32
    ).astype(jnp.bfloat16)
    d_olat = jnp.einsum("qhv,hlv->qhl", d_out, weight_v, preferred_element_type=jnp.float32).astype(
        jnp.bfloat16
    )
    dprob = jnp.einsum("qhl,tl->qht", d_olat, keys_lat, preferred_element_type=jnp.float32)
    delta = jnp.sum(prob * dprob, axis=-1, keepdims=True)
    dscore = (prob * (dprob - delta) * scale).astype(jnp.bfloat16)
    dquery = jnp.einsum("qht,tc->qhc", dscore, keys, preferred_element_type=jnp.float32)
    d_q_rope = dquery[:, :, latent:].astype(jnp.bfloat16)
    d_qlat = dquery[:, :, :latent].astype(jnp.bfloat16)
    d_q_nope = jnp.einsum(
        "qhl,hnl->qhn", d_qlat, weight_k, preferred_element_type=jnp.float32
    ).astype(jnp.bfloat16)
    value_part = jnp.einsum("qht,qhl->tl", prob_low, d_olat, preferred_element_type=jnp.float32)
    dkeys = jnp.einsum("qht,qhc->tc", dscore, qfull, preferred_element_type=jnp.float32)
    dkeys = dkeys + jnp.pad(value_part, ((0, 0), (0, rope)))
    one_hot = (
        asked.reshape(-1)[:, None] == jnp.arange(own_blocks, dtype=jnp.int32)[None, :]
    ).astype(jnp.float32)
    returned = lax.all_to_all(
        dkeys.reshape(peers, per_peer, BLOCK_LEN * width).astype(jnp.bfloat16),
        "seq",
        split_axis=0,
        concat_axis=0,
        tiled=True,
    ).astype(jnp.float32)
    local_grad = jnp.dot(
        one_hot.T,
        returned.reshape(peers * per_peer, BLOCK_LEN * width),
        precision=lax.Precision.HIGHEST,
    )
    d_cache = (
        lax.psum(local_grad.astype(jnp.bfloat16), "grp")
        .astype(jnp.float32)
        .reshape(own_blocks * BLOCK_LEN, width)
    )
    return (attn_out, d_q_nope, d_q_rope, d_cache)


def solution(mesh):
    return jax.shard_map(
        local,
        mesh=mesh,
        in_specs=(
            P("seq", "grp", None),
            P("seq", "grp", None),
            P("seq", None),
            P("grp", "seq"),
            P("grp", "seq"),
            P("seq", "grp", None),
            P("seq", None),
            P("seq", None),
        ),
        out_specs=(
            P("seq", "grp", None),
            P("seq", "grp", None),
            P("seq", "grp", None),
            P("seq", None),
        ),
        check_vma=False,
    )
```

profile of v0, /device:TPU:8, one launch (start us, length us, event | category | flops | bytes accessed | tf_op | source)
XLA Modules:
  0.0 523.4 jit_solution(6179962597997448510)
XLA Ops:
  9.3 12.1 %all-to-all-start = ((s32[64,1,1]{2,1,0:T(1,128)}), s32[64,1,1]{2,1,0:T(1,128)S(1)}, u32[]{:S(2)}, u32[]{:S(2)}) async-start(s32[64,1,1]{2,1,0:T(1,128)} %copy.80), calls=%async_computation | async-start | bytes 65536 | tf_op jit(solution)/shard_map/all_to_all | solution.py:28
  23.1 6.9 %all-to-all-done = s32[64,1,1]{2,1,0:T(1,128)S(1)} async-done(((s32[64,1,1]{2,1,0:T(1,128)}), s32[64,1,1]{2,1,0:T(1,128)S(1)}, u32[]{:S(2)}, u32[]{:S(2)}) %all-to-all-start) | async-done | bytes 288 | tf_op jit(solution)/shard_map/all_to_all | solution.py:28
  32.3 3.5 gather_fusion
  35.8 6.7 %all-to-all-start.1 = ((bf16[64,1,64,576]{3,2,1,0:T(8,128)(2,1)}), bf16[64,1,64,576]{3,2,1,0:T(8,128)(2,1)}, u32[]{:S(2)}, u32[]{:S(2)}) async-start(bf16[64,1,64,576]{3,2,1,0:T(8,128)(2,1)} %bitcast.47), calls=%async_computation.1 | async-start | bytes 10485760 | tf_op jit(solution)/shard_map/all_to_all | solution.py:30
  43.9 67.8 %all-gather.5.cloned.1.call-done = bf16[32,65536]{1,0:T(8,128)(2,1)} async-done(((bf16[32,1024]{1,0:T(8,128)(2,1)}), bf16[32,65536]{1,0:T(8,128)(2,1)}) %all-gather.5.cloned.1.call-update) | async-done | bytes 4194320 | tf_op jit(solution)/shard_map/all_gather | solution.py:23
  111.7 5.1 copy.102
  116.8 78.3 %all-gather.3.cloned.1.call-done = bf16[32,65536]{1,0:T(8,128)(2,1)} async-done(((bf16[32,1024]{1,0:T(8,128)(2,1)}), bf16[32,65536]{1,0:T(8,128)(2,1)}) %all-gather.3.cloned.1.call-update) | async-done | bytes 4194320 | tf_op jit(solution)/shard_map/all_gather | solution.py:22
  195.1 3.9 copy.101
  203.0 8.0 %fusion.12 = f32[16,32,4096]{2,1,0:T(8,128)} fusion(bf16[4096,576]{1,0:T(8,128)(2,1)} %bitcast.5, bf16[16,32,512]{2,0,1:T(8,128)(2,1)S(1)} %fusion.27), kind=kOutput, calls=%fused_computation.20 | convolution fusion | flops 2147483648 | bytes 13107200 | tf_op jit(solution)/shard_map/qhl,tl->qht/dot_general | solution.py:54
  211.0 10.7 %fusion.50 = (f32[16,32]{1,0:T(8,128)S(1)}, f32[16,32,4096]{2,1,0:T(8,128)}) fusion(pred[16,4096]{1,0:T(8,128)(4,1)S(1)} %broadcast_in_dim.25, bf16[4096,576,1]{1,0,2:T(8,128)(2,1)} %bitcast.6, bf16[16,32,576]{2,0,1:T(8,128)(2,1)S(1)} %pad_maximum_fusion), kind=kOutput, calls=%fused_computation.59 | convolution fusion | flops 2424311808 | bytes 13764608 | tf_op jit(solution)/shard_map/sub | solution.py:43
  221.7 9.4 %convolution_bitcast_fusion = f32[4096,512]{0,1:T(8,128)} fusion(bf16[16,32,512]{2,0,1:T(8,128)(2,1)S(1)} %fusion.27, f32[16,32,4096]{2,1,0:T(8,128)} %get-tuple-element.27, f32[16,32]{1,0:T(8,128)S(1)} %get-tuple-element.26), kind=kOutput, calls=%fused_computation.12 | convolution fusion | flops 2151677952 | bytes 17303552 | tf_op jit(solution)/shard_map/qht,qhl->tl/dot_general | solution.py:63
  231.1 18.8 %fusion.2 = bf16[4096,576]{0,1:T(8,128)(2,1)} fusion(f32[4096,512]{0,1:T(8,128)} %convolution_bitcast_fusion, f32[16,32,4096]{2,1,0:T(8,128)} %fusion.12, bf16[16,32,576]{2,0,1:T(8,128)(2,1)S(1)} %pad_maximum_fusion, f32[16,32,4096]{2,1,0:T(8,128)} %get-tuple-element.27, f32[16,32]{1,0:T(8,128)S(1)} %get-tuple-element.26), kind=kOutput, calls=%fused_computation.5 | convolution fusion | flops 2435322368 | bytes 30476288 | tf_op jit(solution)/shard_map/qht,qhc->tc/dot_general | solution.py:64
  249.9 7.6 %copy.91 = bf16[4096,576]{1,0:T(8,128)(2,1)} copy(bf16[4096,576]{0,1:T(8,128)(2,1)} %fusion.2) | data formatting | bytes 9437184 | tf_op jit(solution)/shard_map/convert_element_type | solution.py:70
  257.5 21.7 %convert_element_type.71 = bf16[64,1,36864]{2,1,0:T(2,128)(2,1)} reshape(bf16[4096,576]{1,0:T(8,128)(2,1)} %copy.91) | data formatting | bytes 9437184 | tf_op jit(solution)/shard_map/convert_element_type | solution.py:70
  279.7 29.9 %reduce.4 = bf16[64,36864]{1,0:T(8,128)(2,1)} reduce(bf16[64,1,36864]{2,1,0:T(2,128)(2,1)} %convert_element_type.71, bf16[]{:T(256)} %broadcast.36), dimensions={1}, to_apply=%convert_element_type.71.reduce_sub_computation | reduce | bytes 9437186 | tf_op jit(solution)/shard_map/convert_element_type | solution.py:70
  309.7 8.3 %reshape.84 = bf16[64,2,18432]{2,1,0:T(2,128)(2,1)} reshape(bf16[64,36864]{1,0:T(8,128)(2,1)} %reduce.4) | data formatting | bytes 9437184
  317.9 8.0 %all-to-all-start.2 = ((bf16[64,2,18432]{2,1,0:T(2,128)(2,1)}), bf16[64,2,18432]{2,1,0:T(2,128)(2,1)}, u32[]{:S(2)}, u32[]{:S(2)}) async-start(bf16[64,2,18432]{2,1,0:T(2,128)(2,1)} %reshape.84), calls=%async_computation.2 | async-start | bytes 9437184 | tf_op jit(solution)/shard_map/all_to_all | solution.py:69
  326.2 7.0 %fusion.24 = bf16[16,32,512]{2,1,0:T(8,128)(2,1)S(1)} fusion(bf16[4096,576]{1,0:T(8,128)(2,1)} %bitcast.5, f32[16,32,4096]{2,1,0:T(8,128)} %get-tuple-element.27, f32[16,32]{1,0:T(8,128)S(1)} %get-tuple-element.26), kind=kOutput, calls=%fused_computation.26 | convolution fusion | flops 2151940096 | bytes 13109248 | tf_op jit(solution)/shard_map/qht,tl->qhl/dot_general | solution.py:45
  333.2 100.1 %all-to-all-done.2 = bf16[64,2,18432]{2,1,0:T(2,128)(2,1)} async-done(((bf16[64,2,18432]{2,1,0:T(2,128)(2,1)}), bf16[64,2,18432]{2,1,0:T(2,128)(2,1)}, u32[]{:S(2)}, u32[]{:S(2)}) %all-to-all-start.2) | async-done | bytes 4718624 | tf_op jit(solution)/shard_map/all_to_all | solution.py:69
  433.3 20.2 %reshape.85 = bf16[64,1,36864]{2,1,0:T(2,128)(2,1)} reshape(bf16[64,2,18432]{2,1,0:T(2,128)(2,1)} %all-to-all-done.2) | data formatting | bytes 9437184
  453.4 8.8 %convolution_convert_fusion = bf16[16,36864]{1,0:T(8,128)(2,1)S(1)} fusion(bf16[64,1,36864]{2,1,0:T(2,128)(2,1)} %reshape.85, s32[64]{0:T(128)S(1)} %get-tuple-element.24), kind=kOutput, calls=%fused_computation.3 | convolution fusion | flops 76088320 | bytes 5898496 | tf_op jit(solution)/shard_map/dot_general | solution.py:76
  464.7 14.8 %fusion.21 = bf16[16,32,576]{2,1,0:T(8,128)(2,1)S(1)} fusion(bf16[4096,576,1]{1,0,2:T(8,128)(2,1)} %bitcast.6, f32[16,32,4096]{2,1,0:T(8,128)} %fusion.12, f32[16,32,4096]{2,1,0:T(8,128)} %get-tuple-element.27, f32[16,32]{1,0:T(8,128)S(1)} %get-tuple-element.26), kind=kOutput, calls=%fused_computation.25 | convolution fusion | flops 2430898688 | bytes 22087680 | tf_op jit(solution)/shard_map/qht,tc->qhc/dot_general | solution.py:57
  480.2 3.5 fusion.29
  486.3 27.6 %all-reduce.3.cloned.1.call-done = bf16[1024,576]{1,0:T(8,128)(2,1)} async-done(((bf16[1024,576]{1,0:T(8,128)(2,1)}), bf16[1024,576]{1,0:T(8,128)(2,1)}) %all-reduce.3.cloned.1.call-update) | async-done | bytes 1179664 | tf_op jit(solution)/shard_map/psum | solution.py:82
  (42 shorter events, 20.8 us)
Async XLA Ops:
  7.2 194.6 %copy-start = (bf16[16,32,128]{2,1,0:T(8,128)(2,1)S(1)}, bf16[16,32,128]{2,1,0:T(8,128)(2,1)}, u32[]{:S(2)}) copy-start(bf16[16,32,128]{2,1,0:T(8,128)(2,1)} %param.13) | copy-start | bytes 393220
  7.2 104.5 %all-gather.5.cloned.1.call-start = ((), (), s32[]{:S(2)}) async-start(), calls=%async_computation.4 | async-start | bytes 4259840 | tf_op jit(solution)/shard_map/all_gather | solution.py:23
  9.3 20.7 %all-to-all-start = ((s32[64,1,1]{2,1,0:T(1,128)}), s32[64,1,1]{2,1,0:T(1,128)S(1)}, u32[]{:S(2)}, u32[]{:S(2)}) async-start(s32[64,1,1]{2,1,0:T(1,128)} %copy.80), calls=%async_computation | async-start | bytes 65536 | tf_op jit(solution)/shard_map/all_to_all | solution.py:28
  35.8 7.4 %copy-start.7 = (s32[16,32]{1,0:T(8,128)S(1)}, s32[16,32]{1,0:T(8,128)}, u32[]{:S(2)}) copy-start(s32[16,32]{1,0:T(8,128)} %param.14) | copy-start | bytes 6148
  35.8 8.0 %copy-start.6 = (bf16[16,32,64]{2,1,0:T(8,128)(2,1)S(1)}, bf16[16,32,64]{2,1,0:T(8,128)(2,1)}, u32[]{:S(2)}) copy-start(bf16[16,32,64]{2,1,0:T(8,128)(2,1)} %param.9) | copy-start | bytes 196612
  35.8 167.2 %all-to-all-start.1 = ((bf16[64,1,64,576]{3,2,1,0:T(8,128)(2,1)}), bf16[64,1,64,576]{3,2,1,0:T(8,128)(2,1)}, u32[]{:S(2)}, u32[]{:S(2)}) async-start(bf16[64,1,64,576]{3,2,1,0:T(8,128)(2,1)} %bitcast.47), calls=%async_computation.1 | async-start | bytes 10485760 | tf_op jit(solution)/shard_map/all_to_all | solution.py:30
  42.5 152.7 %all-gather.3.cloned.1.call-start = ((), (), s32[]{:S(2)}) async-start(), calls=%async_computation.3 | async-start | bytes 4259840 | tf_op jit(solution)/shard_map/all_gather | solution.py:22
  116.8 84.3 %copy-start.5 = (bf16[16,32,128]{2,1,0:T(8,128)(2,1)S(1)}, bf16[16,32,128]{2,1,0:T(8,128)(2,1)}, u32[]{:S(2)}) copy-start(bf16[16,32,128]{2,1,0:T(8,128)(2,1)} %param.8) | copy-start | bytes 393220
  195.1 6.7 %copy-start.2 = (bf16[4,8,512,128]{3,2,1,0:T(8,128)(2,1)S(1)}, bf16[4,8,512,128]{3,2,1,0:T(8,128)(2,1)}, u32[]{:S(2)}) copy-start(bf16[4,8,512,128]{3,2,1,0:T(8,128)(2,1)} %copy.102) | copy-start | bytes 12582916
  199.0 2.1 copy-start.3
  317.9 115.3 %all-to-all-start.2 = ((bf16[64,2,18432]{2,1,0:T(2,128)(2,1)}), bf16[64,2,18432]{2,1,0:T(2,128)(2,1)}, u32[]{:S(2)}, u32[]{:S(2)}) async-start(bf16[64,2,18432]{2,1,0:T(2,128)(2,1)} %reshape.84), calls=%async_computation.2 | async-start | bytes 9437184 | tf_op jit(solution)/shard_map/all_to_all | solution.py:69
  325.9 188.0 %all-reduce.3.cloned.1.call-start = ((), (), s32[]{:S(2)}) async-start(), calls=%async_computation.5 | async-start | bytes 2621440 | tf_op jit(solution)/shard_map/psum | solution.py:82
  479.5 5.0 copy-start.4
  480.2 36.4 %copy-start.1 = (bf16[16,32,128]{2,1,0:T(8,128)(2,1)S(1)}, bf16[16,32,128]{2,1,0:T(8,128)(2,1)}, u32[]{:S(2)}) copy-start(bf16[16,32,128]{2,1,0:T(8,128)(2,1)} %param.13) | copy-start | bytes 393220
Sparse Core Ops, SparseCore 0:
  10.8 100.8 all-gather.4
  114.5 80.5 all-gather.2
  464.8 49.0 all-reduce.2
where the time goes:
time: 529 us; the launch traced here: 523 us
  waiting for transfers between devices  282 us (53%)
  matrix products  84 us (16%)
  local copies, waits for them, and re-layouts  83.7 us (16%)
  other arithmetic  32.5 us (6%)
  starting transfers between devices  27.5 us (5%)
  between operations  14.1 us (3%)
    all_to_all x1, waiting for transfers between devices, local(): lax.all_to_all(dkeys.reshape(peers, per_peer, BLOCK_LEN * width).astype(j...  100 us
    all_gather x1, waiting for transfers between devices, local(): lax.all_gather(w_uk, 'seq', axis=1, tiled=True)  78.3 us
    all_gather x1, waiting for transfers between devices, local(): lax.all_gather(w_uv, 'seq', axis=1, tiled=True)  67.8 us
    unnamed x25, local copies, waits for them, and re-layouts  45.4 us
    convert_element_type x1, other arithmetic, local(): dkeys.reshape(peers, per_peer, BLOCK_LEN * width).astype(jnp.bfloat16)  29.9 us
    convert_element_type x3, local copies, waits for them, and re-layouts, local(): dkeys.reshape(peers, per_peer, BLOCK_LEN * width).astype(jnp.bfloat16)  29.9 us
    psum x1, waiting for transfers between devices, local(): lax.psum(local_grad.astype(jnp.bfloat16), 'grp').astype(jnp.float32)  27.6 us
    dot_general x1, matrix products, local(): jnp.einsum('qht,qhc->tc', dscore, qfull, preferred_element_type=jnp.float32)  18.8 us
  transfers between devices with their start and end apart: 6, of which 5 were waited for; matrix products, arithmetic and copies ran while one was open for 9% of the time, Pallas kernels for 0%

commit v1 on v0

--- a/solution.py
+++ b/solution.py
@@ -79,7 +79,7 @@
         precision=lax.Precision.HIGHEST,
     )
     d_cache = (
-        lax.psum(local_grad.astype(jnp.bfloat16), "grp")
+        jnp.sum(lax.all_gather(local_grad.astype(jnp.bfloat16), "grp"), axis=0)
         .astype(jnp.float32)
         .reshape(own_blocks * BLOCK_LEN, width)
     )

time: 529 us -> 539 us (1.019)
  blocking collectives: 0 us -> 115 us
  waiting for transfers between devices: 282 us -> 180 us
  starting transfers between devices: 27.5 us -> 19.2 us
    all_to_all x0 -> x1, blocking collectives: none -> 115 us  [local(): lax.all_to_all(dkeys.reshape(peers, per_peer, BLOCK_LEN * width).astype(j...]
    all_to_all x1 -> x0, waiting for transfers between devices: 100 us -> none  [local(): lax.all_to_all(dkeys.reshape(peers, per_peer, BLOCK_LEN * width).astype(j...]
    psum x1 -> x0, waiting for transfers between devices: 27.6 us -> none  [local(): lax.psum(local_grad.astype(jnp.bfloat16), 'grp').astype(jnp.float32)]
    all_gather x0 -> x1, waiting for transfers between devices: none -> 23.7 us  [local(): lax.all_gather(local_grad.astype(jnp.bfloat16), 'grp')]
    all_to_all x1 -> x0, starting transfers between devices: 7.96 us -> none  [local(): lax.all_to_all(dkeys.reshape(peers, per_peer, BLOCK_LEN * width).astype(j...]
    unnamed x25 -> x27, local copies, waits for them, and re-layouts: 45.4 us -> 45.4 us
  transfers between devices with their start and end apart: 6 -> 5, of which waited for: 5 -> 4; matrix products, arithmetic and copies ran while one was open for 9% -> 9% of each run, Pallas kernels for 0% -> 0%
where the time goes in v1:
time: 539 us; the launch traced here: 533 us
  waiting for transfers between devices  180 us (33%)
  blocking collectives  115 us (21%)
  matrix products  84 us (16%)
  local copies, waits for them, and re-layouts  83.7 us (16%)
  other arithmetic  36.9 us (7%)
  starting transfers between devices  19.2 us (4%)
  between operations  14.1 us (3%)
    all_to_all x1, blocking collectives, local(): lax.all_to_all(dkeys.reshape(peers, per_peer, BLOCK_LEN * width).astype(j...  115 us
    all_gather x1, waiting for transfers between devices, local(): lax.all_gather(w_uk, 'seq', axis=1, tiled=True)  80.1 us
    all_gather x1, waiting for transfers between devices, local(): lax.all_gather(w_uv, 'seq', axis=1, tiled=True)  67.6 us
    unnamed x27, local copies, waits for them, and re-layouts  45.4 us
    convert_element_type x1, other arithmetic, local(): dkeys.reshape(peers, per_peer, BLOCK_LEN * width).astype(jnp.bfloat16)  29.9 us
    convert_element_type x3, local copies, waits for them, and re-layouts, local(): dkeys.reshape(peers, per_peer, BLOCK_LEN * width).astype(jnp.bfloat16)  29.9 us
    all_gather x1, waiting for transfers between devices, local(): lax.all_gather(local_grad.astype(jnp.bfloat16), 'grp')  23.7 us
    dot_general x1, matrix products, local(): jnp.einsum('qht,qhc->tc', dscore, qfull, preferred_element_type=jnp.float32)  18.8 us
  transfers between devices with their start and end apart: 5, of which 4 were waited for; matrix products, arithmetic and copies ran while one was open for 9% of the time, Pallas kernels for 0%

profile of v1, /device:TPU:8, one launch (start us, length us, event | category | flops | bytes accessed | tf_op | source)
XLA Modules:
  0.0 532.9 jit_solution(2566794556627996939)
XLA Ops:
  9.3 12.1 %all-to-all-start = ((s32[64,1,1]{2,1,0:T(1,128)}), s32[64,1,1]{2,1,0:T(1,128)S(1)}, u32[]{:S(2)}, u32[]{:S(2)}) async-start(s32[64,1,1]{2,1,0:T(1,128)} %copy.79), calls=%async_computation | async-start | bytes 65536 | tf_op jit(solution)/shard_map/all_to_all | solution.py:28
  23.1 6.9 %all-to-all-done = s32[64,1,1]{2,1,0:T(1,128)S(1)} async-done(((s32[64,1,1]{2,1,0:T(1,128)}), s32[64,1,1]{2,1,0:T(1,128)S(1)}, u32[]{:S(2)}, u32[]{:S(2)}) %all-to-all-start) | async-done | bytes 288 | tf_op jit(solution)/shard_map/all_to_all | solution.py:28
  32.3 3.5 gather_fusion
  35.8 6.6 %all-to-all-start.1 = ((bf16[64,1,64,576]{3,2,1,0:T(8,128)(2,1)}), bf16[64,1,64,576]{3,2,1,0:T(8,128)(2,1)}, u32[]{:S(2)}, u32[]{:S(2)}) async-start(bf16[64,1,64,576]{3,2,1,0:T(8,128)(2,1)} %bitcast.48), calls=%async_computation.1 | async-start | bytes 10485760 | tf_op jit(solution)/shard_map/all_to_all | solution.py:30
  44.2 67.6 %all-gather.7.cloned.1.call-done = bf16[32,65536]{1,0:T(8,128)(2,1)} async-done(((bf16[32,1024]{1,0:T(8,128)(2,1)}), bf16[32,65536]{1,0:T(8,128)(2,1)}) %all-gather.7.cloned.1.call-update) | async-done | bytes 4194320 | tf_op jit(solution)/shard_map/all_gather | solution.py:23
  111.8 5.2 copy.101
  117.0 80.1 %all-gather.5.cloned.1.call-done = bf16[32,65536]{1,0:T(8,128)(2,1)} async-done(((bf16[32,1024]{1,0:T(8,128)(2,1)}), bf16[32,65536]{1,0:T(8,128)(2,1)}) %all-gather.5.cloned.1.call-update) | async-done | bytes 4194320 | tf_op jit(solution)/shard_map/all_gather | solution.py:22
  197.0 3.9 copy.100
  204.9 8.0 %fusion.12 = f32[16,32,4096]{2,1,0:T(8,128)} fusion(bf16[4096,576]{1,0:T(8,128)(2,1)} %bitcast.5, bf16[16,32,512]{2,0,1:T(8,128)(2,1)S(1)} %fusion.27), kind=kOutput, calls=%fused_computation.20 | convolution fusion | flops 2147483648 | bytes 13107200 | tf_op jit(solution)/shard_map/qhl,tl->qht/dot_general | solution.py:54
  212.9 10.7 %fusion.50 = (f32[16,32]{1,0:T(8,128)S(1)}, f32[16,32,4096]{2,1,0:T(8,128)}) fusion(pred[16,4096]{1,0:T(8,128)(4,1)S(1)} %broadcast_in_dim.25, bf16[4096,576,1]{1,0,2:T(8,128)(2,1)} %bitcast.6, bf16[16,32,576]{2,0,1:T(8,128)(2,1)S(1)} %pad_maximum_fusion), kind=kOutput, calls=%fused_computation.59 | convolution fusion | flops 2424311808 | bytes 13764608 | tf_op jit(solution)/shard_map/sub | solution.py:43
  223.6 9.8 %convolution_bitcast_fusion = f32[4096,512]{0,1:T(8,128)} fusion(bf16[16,32,512]{2,0,1:T(8,128)(2,1)S(1)} %fusion.27, f32[16,32,4096]{2,1,0:T(8,128)} %get-tuple-element.27, f32[16,32]{1,0:T(8,128)S(1)} %get-tuple-element.26), kind=kOutput, calls=%fused_computation.12 | convolution fusion | flops 2151677952 | bytes 17303552 | tf_op jit(solution)/shard_map/qht,qhl->tl/dot_general | solution.py:63
  233.4 18.8 %fusion.2 = bf16[4096,576]{0,1:T(8,128)(2,1)} fusion(f32[4096,512]{0,1:T(8,128)} %convolution_bitcast_fusion, f32[16,32,4096]{2,1,0:T(8,128)} %fusion.12, bf16[16,32,576]{2,0,1:T(8,128)(2,1)S(1)} %pad_maximum_fusion, f32[16,32,4096]{2,1,0:T(8,128)} %get-tuple-element.27, f32[16,32]{1,0:T(8,128)S(1)} %get-tuple-element.26), kind=kOutput, calls=%fused_computation.5 | convolution fusion | flops 2435322368 | bytes 30476288 | tf_op jit(solution)/shard_map/qht,qhc->tc/dot_general | solution.py:64
  252.2 7.6 %copy.90 = bf16[4096,576]{1,0:T(8,128)(2,1)} copy(bf16[4096,576]{0,1:T(8,128)(2,1)} %fusion.2) | data formatting | bytes 9437184 | tf_op jit(solution)/shard_map/convert_element_type | solution.py:70
  259.8 21.7 %convert_element_type.82 = bf16[64,1,36864]{2,1,0:T(2,128)(2,1)} reshape(bf16[4096,576]{1,0:T(8,128)(2,1)} %copy.90) | data formatting | bytes 9437184 | tf_op jit(solution)/shard_map/convert_element_type | solution.py:70
  282.0 29.9 %reduce.5 = bf16[64,36864]{1,0:T(8,128)(2,1)} reduce(bf16[64,1,36864]{2,1,0:T(2,128)(2,1)} %convert_element_type.82, bf16[]{:T(256)} %broadcast.36), dimensions={1}, to_apply=%convert_element_type.82.reduce_sub_computation | reduce | bytes 9437186 | tf_op jit(solution)/shard_map/convert_element_type | solution.py:70
  312.0 8.2 %reshape.82 = bf16[64,2,18432]{2,1,0:T(2,128)(2,1)} reshape(bf16[64,36864]{1,0:T(8,128)(2,1)} %reduce.5) | data formatting | bytes 9437184
  320.2 115.3 %all_to_all.19 = bf16[64,2,18432]{2,1,0:T(2,128)(2,1)} all-to-all(bf16[64,2,18432]{2,1,0:T(2,128)(2,1)} %reshape.82), channel_id=1, replica_groups=mesh['seq'=64,'grp'=4] {'seq'}, dimensions={0} | all-to-all | bytes 9437184 | tf_op jit(solution)/shard_map/all_to_all | solution.py:69
  435.5 20.1 %reshape.83 = bf16[64,1,36864]{2,1,0:T(2,128)(2,1)} reshape(bf16[64,2,18432]{2,1,0:T(2,128)(2,1)} %all_to_all.19) | data formatting | bytes 9437184
  455.7 9.8 %convolution_convert_fusion = bf16[16,36864]{1,0:T(8,128)(2,1)} fusion(bf16[64,1,36864]{2,1,0:T(2,128)(2,1)} %reshape.83, s32[64]{0:T(128)S(1)} %get-tuple-element.24), kind=kOutput, calls=%fused_computation.3 | convolution fusion | flops 76088320 | bytes 5898496 | tf_op jit(solution)/shard_map/dot_general | solution.py:76
  465.5 15.9 %fusion.21 = bf16[16,32,576]{2,1,0:T(8,128)(2,1)S(1)} fusion(bf16[4096,576,1]{1,0,2:T(8,128)(2,1)} %bitcast.6, f32[16,32,4096]{2,1,0:T(8,128)} %fusion.12, f32[16,32,4096]{2,1,0:T(8,128)} %get-tuple-element.27, f32[16,32]{1,0:T(8,128)S(1)} %get-tuple-element.26), kind=kOutput, calls=%fused_computation.25 | convolution fusion | flops 2430898688 | bytes 22087680 | tf_op jit(solution)/shard_map/qht,tc->qhc/dot_general | solution.py:57
  482.1 7.2 %fusion.24 = bf16[16,32,512]{2,1,0:T(8,128)(2,1)S(1)} fusion(bf16[4096,576]{1,0:T(8,128)(2,1)} %bitcast.5, f32[16,32,4096]{2,1,0:T(8,128)} %get-tuple-element.27, f32[16,32]{1,0:T(8,128)S(1)} %get-tuple-element.26), kind=kOutput, calls=%fused_computation.26 | convolution fusion | flops 2151940096 | bytes 13109248 | tf_op jit(solution)/shard_map/qht,tl->qhl/dot_general | solution.py:45
  493.6 23.7 %all-gather.9.cloned.1.call-done = bf16[64,36864]{1,0:T(8,128)(2,1)} async-done(((bf16[16,36864]{1,0:T(8,128)(2,1)}), bf16[64,36864]{1,0:T(8,128)(2,1)}) %all-gather.9.cloned.1.call-update) | async-done | bytes 4718608 | tf_op jit(solution)/shard_map/all_gather | solution.py:82
  517.3 4.4 reduce_sum.32
  521.7 2.4 reshape.65
  (44 shorter events, 19.3 us)
Async XLA Ops:
  7.2 196.6 %copy-start = (bf16[16,32,128]{2,1,0:T(8,128)(2,1)S(1)}, bf16[16,32,128]{2,1,0:T(8,128)(2,1)}, u32[]{:S(2)}) copy-start(bf16[16,32,128]{2,1,0:T(8,128)(2,1)} %param.13) | copy-start | bytes 393220
  7.2 104.6 %all-gather.7.cloned.1.call-start = ((), (), s32[]{:S(2)}) async-start(), calls=%async_computation.4 | async-start | bytes 4259840 | tf_op jit(solution)/shard_map/all_gather | solution.py:23
  9.3 20.7 %all-to-all-start = ((s32[64,1,1]{2,1,0:T(1,128)}), s32[64,1,1]{2,1,0:T(1,128)S(1)}, u32[]{:S(2)}, u32[]{:S(2)}) async-start(s32[64,1,1]{2,1,0:T(1,128)} %copy.79), calls=%async_computation | async-start | bytes 65536 | tf_op jit(solution)/shard_map/all_to_all | solution.py:28
  35.8 7.7 %copy-start.8 = (s32[16,32]{1,0:T(8,128)S(1)}, s32[16,32]{1,0:T(8,128)}, u32[]{:S(2)}) copy-start(s32[16,32]{1,0:T(8,128)} %param.14) | copy-start | bytes 6148
  35.8 8.4 %copy-start.7 = (bf16[16,32,64]{2,1,0:T(8,128)(2,1)S(1)}, bf16[16,32,64]{2,1,0:T(8,128)(2,1)}, u32[]{:S(2)}) copy-start(bf16[16,32,64]{2,1,0:T(8,128)(2,1)} %param.9) | copy-start | bytes 196612
  35.8 169.2 %all-to-all-start.1 = ((bf16[64,1,64,576]{3,2,1,0:T(8,128)(2,1)}), bf16[64,1,64,576]{3,2,1,0:T(8,128)(2,1)}, u32[]{:S(2)}, u32[]{:S(2)}) async-start(bf16[64,1,64,576]{3,2,1,0:T(8,128)(2,1)} %bitcast.48), calls=%async_computation.1 | async-start | bytes 10485760 | tf_op jit(solution)/shard_map/all_to_all | solution.py:30
  42.4 154.6 %all-gather.5.cloned.1.call-start = ((), (), s32[]{:S(2)}) async-start(), calls=%async_computation.3 | async-start | bytes 4259840 | tf_op jit(solution)/shard_map/all_gather | solution.py:22
  43.2 474.1 %all-gather.9.cloned.1.call-start = ((), (), s32[]{:S(2)}) async-start(), calls=%async_computation.5 | async-start | bytes 5898240 | tf_op jit(solution)/shard_map/all_gather | solution.py:82
  117.0 86.0 %copy-start.6 = (bf16[16,32,128]{2,1,0:T(8,128)(2,1)S(1)}, bf16[16,32,128]{2,1,0:T(8,128)(2,1)}, u32[]{:S(2)}) copy-start(bf16[16,32,128]{2,1,0:T(8,128)(2,1)} %param.8) | copy-start | bytes 393220
  197.0 6.7 %copy-start.2 = (bf16[4,8,512,128]{3,2,1,0:T(8,128)(2,1)S(1)}, bf16[4,8,512,128]{3,2,1,0:T(8,128)(2,1)}, u32[]{:S(2)}) copy-start(bf16[4,8,512,128]{3,2,1,0:T(8,128)(2,1)} %copy.101) | copy-start | bytes 12582916
  200.9 2.1 copy-start.4
  482.1 7.2 %copy-start.3 = (bf16[4,8,512,128]{3,2,1,0:T(8,128)(2,1)S(1)}, bf16[4,8,512,128]{3,2,1,0:T(8,128)(2,1)}, u32[]{:S(2)}) copy-start(bf16[4,8,512,128]{3,2,1,0:T(8,128)(2,1)} %copy.101) | copy-start | bytes 12582916
  489.3 2.3 copy-start.5
  517.3 8.8 %copy-start.1 = (bf16[16,32,128]{2,1,0:T(8,128)(2,1)S(1)}, bf16[16,32,128]{2,1,0:T(8,128)(2,1)}, u32[]{:S(2)}) copy-start(bf16[16,32,128]{2,1,0:T(8,128)(2,1)} %param.13) | copy-start | bytes 393220
Sparse Core Ops, SparseCore 0:
  10.8 100.9 all-gather.6
  114.6 82.3 all-gather.4
  465.6 51.6 all-gather.8
